TPU v7x, 256 devices: a whole 4x4x8 slice. The times are simulated.
256 devices in a mesh: samp: 64 (over z, y, core), var: 4 (over x).
Axes of the slice: x: 4, y: 4, z: 8, core: 2. Of those that a mesh axis runs over, the one named last changes fastest.
Arguments:
- dosage: bfloat16 [16384, 40960], P('samp', 'var'), may hold values from 0 to 2
- centers: float32 [40960], replicated, may hold values from 0.4 to 1.34
- scales: float32 [40960], replicated, may hold values from 1.6 to 2.2
- phenotype: float32 [16384], P('samp'), may hold values from -6 to 6
- fold_ids: int32 [16384], P('samp'), may hold values from 0 to 3
- strong_blocks: int32 [32], replicated, may hold values from 0 to 319, as said below
- warm_start: float32 [4096, 32], replicated, may hold values from -4 to 4
- penalty: float32 [8], replicated, may hold values from 0.05 to 0.5
- step_size: float32 [32], replicated, may hold values from 0.2 to 0.6
Outputs:
- margin: float32 [40960], P('var')
- coefficients: float32 [4096, 32], P('var')
Inputs may be any that keep to these rules, and one draw needn't show every extreme that they name: `strong_blocks`: 32 different block numbers.
All inputs are finite; a program needn't handle non-finite values.
Results may differ from a plain program's by a relative error of at most 0.0075.
Values may be sent and summed in bfloat16 or wider, within the bound.
No kernel may reach another device: no remote copies, remote signals or barrier semaphores. Data moves between devices by JAX's collectives and lax.ppermute only.
A program may use at most 64 MiB of HBM per device.

v0:
```python
import math
import jax
import jax.numpy as jnp
from jax import lax
from jax.sharding import PartitionSpec as P

BLOCK = 128
NS = 4096
LAMBDAS = 8
FOLDS = 4
ITERS = 3
exact_mode = lax.Precision.HIGHEST


def shards(
    dosage, centers, scales, phenotype, fold_ids, strong_blocks, warm_start, penalty, step_size
):
    rows, local_width = dosage.shape
    groups = lax.axis_size("var")
    place = lax.axis_index("var")
    fit_total = LAMBDAS * FOLDS
    fit_folds = jnp.arange(fit_total, dtype=jnp.int32) % FOLDS
    weights = (fold_ids[:, None] != fit_folds[None, :]).astype(jnp.float32)
    counts = lax.psum(jnp.sum(weights, axis=0), "samp")
    fit_penalty = jnp.repeat(penalty, FOLDS)
    threshold = step_size * fit_penalty
    local_blocks = local_width // BLOCK
    relative = strong_blocks - place * local_blocks
    owned = (relative >= 0) & (relative < local_blocks)
    picked = jnp.take(
        dosage.reshape(rows, local_blocks, BLOCK), jnp.clip(relative, 0, local_blocks - 1), axis=1
    )
    masked = (picked * owned.astype(jnp.bfloat16)[None, :, None]).reshape(rows, NS)
    columns = (
        strong_blocks[:, None] * BLOCK + jnp.arange(BLOCK, dtype=jnp.int32)[None, :]
    ).reshape(NS)
    strong_centers = centers[columns]
    strong_scales = scales[columns]
    owned_columns = jnp.repeat(owned.astype(jnp.float32), BLOCK)
    share = NS // groups
    point = warm_start
    part_centers = strong_centers * owned_columns
    part_threshold = threshold[None, :]

    def residual_of(coef):
        scaled = (strong_scales[:, None] * coef).astype(jnp.bfloat16)
        partial_fit = jnp.dot(masked, scaled, preferred_element_type=jnp.float32)
        partial_fit = (
            partial_fit - jnp.dot(part_centers * strong_scales, coef, precision=exact_mode)[None, :]
        )
        fitted = lax.psum(partial_fit.astype(jnp.bfloat16), "var").astype(jnp.float32)
        return (weights * (phenotype[:, None] - fitted)).astype(jnp.bfloat16)

    rounded = residual_of(point)
    column_sums = jnp.sum(rounded.astype(jnp.float32), axis=0)
    local_centers = lax.dynamic_slice_in_dim(centers, place * local_width, local_width, 0)
    local_scales = lax.dynamic_slice_in_dim(scales, place * local_width, local_width, 0)
    cross = lax.dot_general(
        dosage, rounded, (((0,), (0,)), ((), ())), preferred_element_type=jnp.float32
    )
    total = lax.psum(cross - local_centers[:, None] * column_sums[None, :], "samp")
    margin = jnp.max(
        jnp.abs(local_scales[:, None] * total / counts[None, :]) / fit_penalty[None, :], axis=1
    )
    momentum = 1.0
    previous = point
    for sweep in range(ITERS):
        if sweep > 0:
            rounded = residual_of(point)
            column_sums = jnp.sum(rounded.astype(jnp.float32), axis=0)
        gradient_cross = lax.dot_general(
            masked, rounded, (((0,), (0,)), ((), ())), preferred_element_type=jnp.float32
        )
        gradient_cross = gradient_cross - part_centers[:, None] * column_sums[None, :]
        gradient_total = lax.psum(gradient_cross, ("samp", "var"))
        moved = point + step_size[None, :] * (
            strong_scales[:, None] * gradient_total / counts[None, :]
        )
        current = moved - jnp.clip(moved, -part_threshold, part_threshold)
        following = (1.0 + math.sqrt(1.0 + 4.0 * momentum * momentum)) / 2.0
        point = current + (momentum - 1.0) / following * (current - previous)
        previous = current
        momentum = following
    coefficients = lax.dynamic_slice_in_dim(previous, place * share, share, 0)
    return (margin, coefficients)


def solution(mesh):
    return jax.shard_map(
        shards,
        mesh=mesh,
        in_specs=(P("samp", "var"), P(), P(), P("samp"), P("samp"), P(), P(), P(), P()),
        out_specs=(P("var"), P("var", None)),
        check_vma=False,
    )
```

profile of v0, /device:TPU:2, one launch (start us, length us, event | category | flops | bytes accessed | tf_op | source)
XLA Modules:
  0.0 1087.9 jit_solution(17105678928884932665)
XLA Ops:
  7.2 0.0 all-reduce.7.cloned.1.call-start
  7.2 7.9 copy.11
  15.2 7.9 copy.12
  23.1 3.4 gather_fusion
  26.6 2.9 copy.13
  29.5 0.1 broadcast_bitcast_fusion
  29.6 0.1 broadcast_bitcast_fusion.1
  29.7 0.1 iota_add_fusion
  29.8 23.0 %gather_fusion.1 = f32[4096]{0:T(1024)S(1)} fusion(f32[40960]{0:T(1024)S(1)} %copy-done.1, s32[4096]{0:T(1024)S(1)} %broadcast_clamp_fusion), kind=kCustom, calls=%fused_computation.1 | custom fusion | bytes 49152 | tf_op jit(solution)/shard_map/gather | solution.py:38
  52.9 23.0 %gather_fusion.2 = f32[4096]{0:T(1024)S(1)} fusion(f32[40960]{0:T(1024)S(1)} %copy-done, s32[4096]{0:T(1024)S(1)} %broadcast_clamp_fusion), kind=kCustom, calls=%fused_computation.2 | custom fusion | bytes 49152 | tf_op jit(solution)/shard_map/gather | solution.py:37
  75.9 0.1 fusion.23
  76.0 0.5 convolution_bitcast_fusion.3
  76.5 3.2 fusion.1
  79.7 0.4 fusion.3
  80.2 15.3 %psum.56 = bf16[256,32]{0,1:T(8,128)(2,1)S(1)} all-reduce(bf16[256,32]{0,1:T(8,128)(2,1)S(1)} %fusion.3), channel_id=1, replica_groups=mesh['samp'=64,'var'=4] {'var'}, use_global_device_ids=true, to_apply=%region_0.1 | all-reduce | flops 8192 | bytes 32768 | tf_op jit(solution)/shard_map/psum | solution.py:51
  95.5 0.2 fusion.11
  95.7 1.5 convolution_subtract_fusion.2
  97.2 0.0 all-reduce.7.cloned.1.call-update
  97.2 0.0 all-reduce.9.cloned.1.call-start
  97.3 0.1 broadcast_in_dim.26
  97.4 0.1 div.40
  97.4 127.1 %psum.58 = f32[32]{0:T(128)S(1)} all-reduce(f32[32]{0:T(128)S(1)} %get-tuple-element.2), channel_id=1, replica_groups=mesh['samp'=64,'var'=4] {'samp'}, use_global_device_ids=true, to_apply=%region_4.5 | all-reduce | flops 32 | bytes 256 | tf_op jit(solution)/shard_map/psum | solution.py:24
  224.5 131.6 %all-reduce.7.cloned.1.call-done = f32[4096,32]{0,1:T(8,128)} async-done(((f32[4096,32]{0,1:T(8,128)}), f32[4096,32]{0,1:T(8,128)}) %all-reduce.7.cloned.1.call-update) | async-done | bytes 524304 | tf_op jit(solution)/shard_map/psum | solution.py:75
  356.1 1.8 convolution_bitcast_fusion.2
  357.9 0.5 fusion.4
  358.5 0.0 dynamic-slice-start
  358.5 14.0 %psum.60 = bf16[256,32]{0,1:T(8,128)(2,1)S(1)} all-reduce(bf16[256,32]{0,1:T(8,128)(2,1)S(1)} %fusion.4), channel_id=1, replica_groups=mesh['samp'=64,'var'=4] {'var'}, use_global_device_ids=true, to_apply=%region_7.8 | all-reduce | flops 8192 | bytes 32768 | tf_op jit(solution)/shard_map/psum | solution.py:51
  372.5 0.2 convert_reduce_fusion.1
  372.7 1.5 convolution_subtract_fusion.1
  374.2 0.0 all-reduce.9.cloned.1.call-update
  374.3 0.0 all-reduce.5.cloned.1.call-start
  374.3 4.6 fusion
  379.0 0.0 all-reduce.5.cloned.1.call-update
  379.0 0.0 all-reduce.11.cloned.1.call-start
  379.0 250.2 %all-reduce.9.cloned.1.call-done = f32[4096,32]{0,1:T(8,128)} async-done(((f32[4096,32]{0,1:T(8,128)}), f32[4096,32]{0,1:T(8,128)}) %all-reduce.9.cloned.1.call-update) | async-done | bytes 524304 | tf_op jit(solution)/shard_map/psum | solution.py:75
  629.3 1.6 multiply_add_fusion
  630.9 0.5 convolution_bitcast_fusion.1
  631.4 0.4 fusion.5
  631.9 0.0 dynamic-slice-start.1
  631.9 13.9 %psum.62 = bf16[256,32]{0,1:T(8,128)(2,1)S(1)} all-reduce(bf16[256,32]{0,1:T(8,128)(2,1)S(1)} %fusion.5), channel_id=1, replica_groups=mesh['samp'=64,'var'=4] {'var'}, use_global_device_ids=true, to_apply=%region_10.11 | all-reduce | flops 8192 | bytes 32768 | tf_op jit(solution)/shard_map/psum | solution.py:51
  645.8 0.2 convert_reduce_fusion
  646.0 1.5 convolution_subtract_fusion
  647.5 0.0 all-reduce.11.cloned.1.call-update
  647.5 172.9 %all-reduce.5.cloned.1.call-done = f32[10240,32]{0,1:T(8,128)} async-done(((f32[10240,32]{0,1:T(8,128)}), f32[10240,32]{0,1:T(8,128)}) %all-reduce.5.cloned.1.call-update) | async-done | bytes 1310736 | tf_op jit(solution)/shard_map/psum | solution.py:61
  820.4 2.3 fusion.2
  822.7 256.9 %all-reduce.11.cloned.1.call-done = f32[4096,32]{0,1:T(8,128)} async-done(((f32[4096,32]{0,1:T(8,128)}), f32[4096,32]{0,1:T(8,128)}) %all-reduce.11.cloned.1.call-update) | async-done | bytes 524304 | tf_op jit(solution)/shard_map/psum | solution.py:75
  1079.6 1.1 broadcast_multiply_fusion
  1080.6 0.8 minimum_subtract_fusion.1
  (32 shorter events, 0.1 us)
Async XLA Ops:
  7.2 348.9 %all-reduce.7.cloned.1.call-start = ((), (), s32[]{:S(2)}) async-start(), calls=%async_computation.1 | async-start | bytes 1048576 | tf_op jit(solution)/shard_map/psum | solution.py:75
  15.2 7.9 copy-start.10
  26.6 3.2 copy-start.1
  29.8 23.1 %copy-start = (f32[40960]{0:T(1024)S(1)}, f32[40960]{0:T(1024)}, u32[]{:S(2)}) copy-start(f32[40960]{0:T(1024)} %param.10) | copy-start | bytes 491524
  52.8 23.1 %copy-start.2 = (f32[4096,32]{0,1:T(8,128)S(1)}, f32[4096,32]{0,1:T(8,128)}, u32[]{:S(2)}) copy-start(f32[4096,32]{0,1:T(8,128)} %param.15) | copy-start | bytes 1572868
  79.7 15.8 %copy-start.4 = (s32[256]{0:T(256)S(1)}, s32[256]{0:T(256)}, u32[]{:S(2)}) copy-start(s32[256]{0:T(256)} %param.13) | copy-start | bytes 3076
  79.7 15.8 %copy-start.5 = (f32[256]{0:T(256)S(1)}, f32[256]{0:T(256)}, u32[]{:S(2)}) copy-start(f32[256]{0:T(256)} %param.12) | copy-start | bytes 3076
  80.1 17.1 %copy-start.9 = (f32[8]{0:T(128)S(1)}, f32[8]{0:T(128)}, u32[]{:S(2)}) copy-start(f32[8]{0:T(128)} %param.16) | copy-start | bytes 100
  80.2 144.4 %copy-start.6 = (f32[32]{0:T(128)S(1)}, f32[32]{0:T(128)}, u32[]{:S(2)}) copy-start(f32[32]{0:T(128)} %param.17) | copy-start | bytes 388
  95.7 128.9 %copy-start.7 = (f32[32]{0:T(128)}, f32[32]{0:T(128)S(1)}, u32[]{:S(2)}) copy-start(f32[32]{0:T(128)S(1)} %get-tuple-element.3) | copy-start | bytes 388
  97.2 532.1 %all-reduce.9.cloned.1.call-start = ((), (), s32[]{:S(2)}) async-start(), calls=%async_computation.2 | async-start | bytes 1048576 | tf_op jit(solution)/shard_map/psum | solution.py:75
  356.1 1.8 copy-start.3
  358.5 15.9 %dynamic-slice-start = ((f32[40960]{0:T(1024)}, s32[]{:T(128)}), f32[10240]{0:T(1024)S(1)}, s32[]{:S(2)}) async-start(f32[40960]{0:T(1024)} %param.10, s32[]{:T(128)} %select_n.39), calls=%async_computation.4 | async-start | bytes 82432 | tf_op jit(solution)/shard_map/dynamic_slice | solution.py:56
  358.5 15.9 %copy-start.8 = (f32[32]{0:T(128)S(1)}, f32[32]{0:T(128)}, u32[]{:S(2)}) copy-start(f32[32]{0:T(128)} %copy-done.7) | copy-start | bytes 388
  374.3 446.2 %all-reduce.5.cloned.1.call-start = ((), (), s32[]{:S(2)}) async-start(), calls=%async_computation | async-start | bytes 2621440 | tf_op jit(solution)/shard_map/psum | solution.py:61
  379.0 700.6 %all-reduce.11.cloned.1.call-start = ((), (), s32[]{:S(2)}) async-start(), calls=%async_computation.3 | async-start | bytes 1048576 | tf_op jit(solution)/shard_map/psum | solution.py:75
  631.9 188.6 %dynamic-slice-start.1 = ((f32[40960]{0:T(1024)}, s32[]{:T(128)}), f32[10240]{0:T(1024)S(1)}, s32[]{:S(2)}) async-start(f32[40960]{0:T(1024)} %param.11, s32[]{:T(128)} %select_n.39), calls=%async_computation.5 | async-start | bytes 82432 | tf_op jit(solution)/shard_map/dynamic_slice | solution.py:57
Sparse Core Ops, SparseCore 0:
  97.3 258.7 all-reduce.6
  374.4 254.8 all-reduce.8
  632.7 187.6 all-reduce.4
  825.7 253.7 all-reduce.10
where the time goes:
time: 1090 us
  waiting for transfers between devices  812 us (74%)
  blocking collectives  170 us (16%)
  local copies, waits for them, and re-layouts  68.7 us (6%)
  between operations  14 us (1%)
  matrix products  13.4 us (1%)
    psum x3, waiting for transfers between devices, shards(): gradient_total = lax.psum(gradient_cross, ('samp', 'var'))  639 us
    psum x1, waiting for transfers between devices, shards(): lax.psum(cross - local_centers[:, None] * column_sums[None, :], 'samp')  173 us
    psum x1, blocking collectives, shards(): counts = lax.psum(jnp.sum(weights, axis=0), 'samp')  127 us
    psum x3, blocking collectives, residual_of(): lax.psum(partial_fit.astype(jnp.bfloat16), 'var').astype(jnp.float32)  43.3 us
    gather x1, local copies, waits for them, and re-layouts, shards(): strong_scales = scales[columns]  23 us
    gather x1, local copies, waits for them, and re-layouts, shards(): strong_centers = centers[columns]  23 us
  transfers between devices with their start and end apart: 4, of which 4 were waited for; matrix products, arithmetic and copies ran while one was open for 1% of the time, Pallas kernels for 0%

commit v1 on v0

--- a/solution.py
+++ b/solution.py
@@ -72,7 +72,7 @@
             masked, rounded, (((0,), (0,)), ((), ())), preferred_element_type=jnp.float32
         )
         gradient_cross = gradient_cross - part_centers[:, None] * column_sums[None, :]
-        gradient_total = lax.psum(gradient_cross, ("samp", "var"))
+        gradient_total = lax.psum(lax.psum(gradient_cross, "var"), "samp")
         moved = point + step_size[None, :] * (
             strong_scales[:, None] * gradient_total / counts[None, :]
         )

time: 1090 us -> 859 us (0.79)
  waiting for transfers between devices: 812 us -> 580 us
    psum x3 -> x5, waiting for transfers between devices: 639 us -> 385 us  [shards(): gradient_total = lax.psum(lax.psum(gradient_cross, 'var'), 'samp')]
    psum x1, waiting for transfers between devices: 173 us -> 195 us  [shards(): lax.psum(cross - local_centers[:, None] * column_sums[None, :], 'samp')]
  transfers between devices with their start and end apart: 4 -> 6, of which waited for: 4 -> 6; matrix products, arithmetic and copies ran while one was open for 1% -> 1% of each run, Pallas kernels for 0% -> 0%
where the time goes in v1:
time: 859 us
  waiting for transfers between devices  580 us (68%)
  blocking collectives  171 us (20%)
  local copies, waits for them, and re-layouts  68.7 us (8%)
  matrix products  14.6 us (2%)
  between operations  14.4 us (2%)
  other arithmetic  10.3 us (1%)
    psum x5, waiting for transfers between devices, shards(): gradient_total = lax.psum(lax.psum(gradient_cross, 'var'), 'samp')  385 us
    psum x1, waiting for transfers between devices, shards(): lax.psum(cross - local_centers[:, None] * column_sums[None, :], 'samp')  195 us
    psum x1, blocking collectives, shards(): counts = lax.psum(jnp.sum(weights, axis=0), 'samp')  127 us
    psum x3, blocking collectives, residual_of(): lax.psum(partial_fit.astype(jnp.bfloat16), 'var').astype(jnp.float32)  43.8 us
    gather x1, local copies, waits for them, and re-layouts, shards(): strong_scales = scales[columns]  23 us
    gather x1, local copies, waits for them, and re-layouts, shards(): strong_centers = centers[columns]  23 us
  transfers between devices with their start and end apart: 6, of which 6 were waited for; matrix products, arithmetic and copies ran while one was open for 1% of the time, Pallas kernels for 0%

profile of v1, /device:TPU:2, one launch (start us, length us, event | category | flops | bytes accessed | tf_op | source)
XLA Modules:
  0.0 858.6 jit_solution(11217240243256080008)
XLA Ops:
  7.2 0.0 all-reduce.8.cloned.1.call-start
  7.2 7.9 copy.11
  15.2 7.9 copy.12
  23.1 3.4 gather_fusion
  26.6 2.9 copy.13
  29.5 0.1 broadcast_bitcast_fusion
  29.6 0.1 broadcast_bitcast_fusion.1
  29.7 0.1 iota_add_fusion
  29.8 23.0 %gather_fusion.1 = f32[4096]{0:T(1024)S(1)} fusion(f32[40960]{0:T(1024)S(1)} %copy-done.1, s32[4096]{0:T(1024)S(1)} %broadcast_clamp_fusion), kind=kCustom, calls=%fused_computation.1 | custom fusion | bytes 49152 | tf_op jit(solution)/shard_map/gather | solution.py:38
  52.9 23.0 %gather_fusion.2 = f32[4096]{0:T(1024)S(1)} fusion(f32[40960]{0:T(1024)S(1)} %copy-done, s32[4096]{0:T(1024)S(1)} %broadcast_clamp_fusion), kind=kCustom, calls=%fused_computation.2 | custom fusion | bytes 49152 | tf_op jit(solution)/shard_map/gather | solution.py:37
  75.9 0.1 fusion.23
  76.0 0.5 convolution_bitcast_fusion.3
  76.5 3.2 fusion.1
  79.7 0.4 fusion.3
  80.2 15.3 %psum.77 = bf16[256,32]{0,1:T(8,128)(2,1)S(1)} all-reduce(bf16[256,32]{0,1:T(8,128)(2,1)S(1)} %fusion.3), channel_id=1, replica_groups=mesh['samp'=64,'var'=4] {'var'}, use_global_device_ids=true, to_apply=%region_0.1 | all-reduce | flops 8192 | bytes 32768 | tf_op jit(solution)/shard_map/psum | solution.py:51
  95.5 0.2 fusion.11
  95.7 1.5 convolution_subtract_fusion.2
  97.2 0.0 all-reduce.8.cloned.1.call-update
  97.2 0.0 all-reduce.10.cloned.1.call-start
  97.3 49.8 %all-reduce.8.cloned.1.call-done = f32[4096,32]{0,1:T(8,128)} async-done(((f32[4096,32]{0,1:T(8,128)}), f32[4096,32]{0,1:T(8,128)}) %all-reduce.8.cloned.1.call-update) | async-done | bytes 524304 | tf_op jit(solution)/shard_map/psum | solution.py:75
  147.1 0.0 all-reduce.12.cloned.1.call-start
  147.2 0.1 broadcast_in_dim.26
  147.3 0.1 div.40
  147.4 127.0 %psum.79 = f32[32]{0:T(128)S(1)} all-reduce(f32[32]{0:T(128)S(1)} %get-tuple-element.2), channel_id=1, replica_groups=mesh['samp'=64,'var'=4] {'samp'}, use_global_device_ids=true, to_apply=%region_4.5 | all-reduce | flops 32 | bytes 256 | tf_op jit(solution)/shard_map/psum | solution.py:24
  274.3 0.6 fusion.22
  274.9 60.9 %all-reduce.10.cloned.1.call-done = f32[4096,32]{0,1:T(8,128)} async-done(((f32[4096,32]{0,1:T(8,128)}), f32[4096,32]{0,1:T(8,128)}) %all-reduce.10.cloned.1.call-update) | async-done | bytes 524304 | tf_op jit(solution)/shard_map/psum | solution.py:75
  335.8 1.8 convolution_bitcast_fusion.2
  337.7 1.8 fusion.4
  339.4 14.5 %psum.82 = bf16[256,32]{0,1:T(8,128)(2,1)S(1)} all-reduce(bf16[256,32]{0,1:T(8,128)(2,1)} %fusion.4), channel_id=1, replica_groups=mesh['samp'=64,'var'=4] {'var'}, use_global_device_ids=true, to_apply=%region_8.9 | all-reduce | flops 8192 | bytes 32768 | tf_op jit(solution)/shard_map/psum | solution.py:51
  354.0 0.2 convert_reduce_fusion.1
  354.2 1.5 convolution_subtract_fusion.1
  355.7 0.0 all-reduce.14.cloned.1.call-start
  355.8 45.1 %all-reduce.12.cloned.1.call-done = f32[4096,32]{0,1:T(8,128)} async-done(((f32[4096,32]{0,1:T(8,128)}), f32[4096,32]{0,1:T(8,128)}) %all-reduce.12.cloned.1.call-update) | async-done | bytes 524304 | tf_op jit(solution)/shard_map/psum | solution.py:75
  400.9 0.0 all-reduce.16.cloned.1.call-start
  401.0 188.3 %all-reduce.14.cloned.1.call-done = f32[4096,32]{0,1:T(8,128)} async-done(((f32[4096,32]{0,1:T(8,128)}), f32[4096,32]{0,1:T(8,128)}) %all-reduce.14.cloned.1.call-update) | async-done | bytes 524304 | tf_op jit(solution)/shard_map/psum | solution.py:75
  589.3 1.6 multiply_add_fusion
  590.9 0.5 convolution_bitcast_fusion.1
  591.4 0.4 fusion.5
  591.9 13.9 %psum.85 = bf16[256,32]{0,1:T(8,128)(2,1)S(1)} all-reduce(bf16[256,32]{0,1:T(8,128)(2,1)S(1)} %fusion.5), channel_id=1, replica_groups=mesh['samp'=64,'var'=4] {'var'}, use_global_device_ids=true, to_apply=%region_12.13 | all-reduce | flops 8192 | bytes 32768 | tf_op jit(solution)/shard_map/psum | solution.py:51
  605.8 0.2 convert_reduce_fusion
  606.0 1.5 convolution_subtract_fusion
  607.5 0.0 all-reduce.18.cloned.1.call-start
  607.6 4.6 fusion
  612.2 40.4 %all-reduce.16.cloned.1.call-done = f32[4096,32]{0,1:T(8,128)} async-done(((f32[4096,32]{0,1:T(8,128)}), f32[4096,32]{0,1:T(8,128)}) %all-reduce.16.cloned.1.call-update) | async-done | bytes 524304 | tf_op jit(solution)/shard_map/psum | solution.py:75
  652.7 194.9 %all-reduce.18.cloned.1.call-done = (f32[10240,32]{0,1:T(8,128)}, f32[4096,32]{0,1:T(8,128)}) async-done(((f32[10240,32]{0,1:T(8,128)}, f32[4096,32]{0,1:T(8,128)}), (f32[10240,32]{0,1:T(8,128)}, f32[4096,32]{0,1:T(8,128)})) %all-reduce.18.cloned.1.call-update) | async-done | bytes 1835024 | tf_op jit(solution)/shard_map/psum | solution.py:61
  847.6 1.1 broadcast_multiply_fusion
  848.7 2.3 fusion.2
  851.0 0.8 minimum_subtract_fusion.1
  (51 shorter events, 0.3 us)
Async XLA Ops:
  7.2 140.0 %all-reduce.8.cloned.1.call-start = ((), (), s32[]{:S(2)}) async-start(), calls=%async_computation | async-start | bytes 1048576 | tf_op jit(solution)/shard_map/psum | solution.py:75
  15.2 7.9 copy-start.17
  26.6 3.2 copy-start.1
  29.8 23.1 %copy-start = (f32[40960]{0:T(1024)S(1)}, f32[40960]{0:T(1024)}, u32[]{:S(2)}) copy-start(f32[40960]{0:T(1024)} %param.10) | copy-start | bytes 491524
  52.8 23.1 %copy-start.2 = (f32[4096,32]{0,1:T(8,128)S(1)}, f32[4096,32]{0,1:T(8,128)}, u32[]{:S(2)}) copy-start(f32[4096,32]{0,1:T(8,128)} %param.15) | copy-start | bytes 1572868
  79.7 15.8 %copy-start.4 = (s32[256]{0:T(256)S(1)}, s32[256]{0:T(256)}, u32[]{:S(2)}) copy-start(s32[256]{0:T(256)} %param.13) | copy-start | bytes 3076
  79.7 15.8 %copy-start.5 = (f32[256]{0:T(256)S(1)}, f32[256]{0:T(256)}, u32[]{:S(2)}) copy-start(f32[256]{0:T(256)} %param.12) | copy-start | bytes 3076
  80.1 67.1 %copy-start.16 = (f32[8]{0:T(128)S(1)}, f32[8]{0:T(128)}, u32[]{:S(2)}) copy-start(f32[8]{0:T(128)} %param.16) | copy-start | bytes 100
  80.2 194.2 %copy-start.6 = (f32[32]{0:T(128)S(1)}, f32[32]{0:T(128)}, u32[]{:S(2)}) copy-start(f32[32]{0:T(128)} %param.17) | copy-start | bytes 388
  95.7 51.5 %copy-start.14 = (f32[32]{0:T(128)}, f32[32]{0:T(128)S(1)}, u32[]{:S(2)}) copy-start(f32[32]{0:T(128)S(1)} %get-tuple-element.3) | copy-start | bytes 388
  97.2 238.6 %all-reduce.10.cloned.1.call-start = ((), (), s32[]{:S(2)}) async-start(), calls=%async_computation.1 | async-start | bytes 1048576 | tf_op jit(solution)/shard_map/psum | solution.py:75
  147.1 253.8 %all-reduce.12.cloned.1.call-start = ((), (), s32[]{:S(2)}) async-start(), calls=%async_computation.2 | async-start | bytes 1048576 | tf_op jit(solution)/shard_map/psum | solution.py:75
  147.4 127.6 %copy-start.12 = (f32[32]{0:T(128)}, f32[32]{0:T(128)S(1)}, u32[]{:S(2)}) copy-start(f32[32]{0:T(128)S(1)} %div.40) | copy-start | bytes 388
  335.8 1.8 copy-start.3
  335.8 1.8 copy-start.8
  335.8 1.8 copy-start.10
  355.7 233.5 %all-reduce.14.cloned.1.call-start = ((), (), s32[]{:S(2)}) async-start(), calls=%async_computation.3 | async-start | bytes 1048576 | tf_op jit(solution)/shard_map/psum | solution.py:75
  400.9 251.7 %all-reduce.16.cloned.1.call-start = ((), (), s32[]{:S(2)}) async-start(), calls=%async_computation.4 | async-start | bytes 1048576 | tf_op jit(solution)/shard_map/psum | solution.py:75
  591.9 15.7 %copy-start.15 = (f32[32]{0:T(128)S(1)}, f32[32]{0:T(128)}, u32[]{:S(2)}) copy-start(f32[32]{0:T(128)} %copy-done.14) | copy-start | bytes 388
  607.5 240.1 %all-reduce.18.cloned.1.call-start = ((), (), s32[]{:S(2)}) async-start(), calls=%async_computation.5 | async-start | bytes 3670016 | tf_op jit(solution)/shard_map/psum | solution.py:61
  612.2 236.5 %dynamic-slice-start = ((f32[40960]{0:T(1024)}, s32[]{:T(128)}), f32[10240]{0:T(1024)S(1)}, s32[]{:S(2)}) async-start(f32[40960]{0:T(1024)} %param.11, s32[]{:T(128)} %select_n.39), calls=%async_computation.6 | async-start | bytes 82432 | tf_op jit(solution)/shard_map/dynamic_slice | solution.py:57
  612.2 236.5 %copy-start.13 = (f32[32]{0:T(128)S(1)}, f32[32]{0:T(128)}, u32[]{:S(2)}) copy-start(f32[32]{0:T(128)} %copy-done.12) | copy-start | bytes 388
  652.6 198.3 %copy-start.7 = (f32[32]{0:T(128)S(1)}, f32[32]{0:T(128)}, u32[]{:S(2)}) copy-start(f32[32]{0:T(128)} %param.17) | copy-start | bytes 388
  652.6 198.3 %copy-start.9 = (f32[32]{0:T(128)S(1)}, f32[32]{0:T(128)}, u32[]{:S(2)}) copy-start(f32[32]{0:T(128)} %get-tuple-element.6) | copy-start | bytes 388
  652.7 198.3 %copy-start.11 = (f32[32]{0:T(128)S(1)}, f32[32]{0:T(128)}, u32[]{:S(2)}) copy-start(f32[32]{0:T(128)} %get-tuple-element.7) | copy-start | bytes 388
Sparse Core Ops, SparseCore 0:
  97.3 49.7 all-reduce.7
  150.6 185.1 all-reduce.9
  355.8 45.0 all-reduce.11
  404.2 184.9 all-reduce.13
  607.6 44.9 all-reduce.15
  656.0 191.5 all-reduce.17
